TPU v7x, 32 devices: a whole 2x2x4 slice. The times are simulated.
32 devices in a mesh: row: 4 (over y, x), col: 8 (over z, core).
Axes of the slice: x: 2, y: 2, z: 4, core: 2. Of those that a mesh axis runs over, the one named last changes fastest.
Arguments:
- tiles: float32 [384, 1024, 128], P('row', 'col'), may hold values from -0.1875 to 0.1875
- tile_row: int32 [384, 8], P('row', 'col'), may hold values from 0 to 511
- tile_col: int32 [384, 8], P('row', 'col'), may hold values from 0 to 255
- tile_count: int32 [4, 8], P('row', 'col'), may hold values from 24 to 96, as said below
- cost: float32 [8, 32768], P('col', 'row'), may hold values from -6 to 6
- rhs: float32 [4, 65536], P('row', 'col'), may hold values from -6 to 6
- lower: float32 [8, 32768], P('col', 'row'), may hold values from -2 to -0.3
- upper: float32 [8, 32768], P('col', 'row'), may hold values from 0.3 to 2
- primal_start: float32 [8, 32768], P('col', 'row'), may hold values from -0.3 to 0.3
- dual_start: float32 [4, 65536], P('row', 'col'), may hold values from 0 to 1
Outputs:
- primal_mean: float32 [8, 32768], P('col', 'row')
- dual_mean: float32 [4, 65536], P('row', 'col')
- primal_last: float32 [8, 32768], P('col', 'row')
- dual_last: float32 [4, 65536], P('row', 'col')
Inputs may be any that keep to these rules, and one draw needn't show every extreme that they name: `tile_count`: live tiles of each device; some device holds 96.
All inputs are finite; a program needn't handle non-finite values.
Results may differ from a plain program's by a relative error of at most 0.0001.
Values sent between devices are 32-bit elements; how exact they have to be, the bound alone decides.
A program may use at most 64 MiB of HBM per device.

v0:
```python
import jax
import jax.numpy as jnp
from jax import lax
from jax.sharding import PartitionSpec as P

ITERS = 6
exact = lax.Precision.HIGHEST
primal_step = 0.3
dual_step = 0.3


def body(tiles, tile_row, tile_col, tile_count, cost, rhs, lower, upper, primal_start, dual_start):
    tile_slots = tiles.shape[0]
    block_size = tiles.shape[2]
    row_blocks = rhs.shape[1] * lax.axis_size("col") // block_size
    col_blocks = cost.shape[1] * lax.axis_size("row") // block_size
    live = (lax.iota(jnp.int32, tile_slots) < tile_count.reshape(())).astype(jnp.float32)
    row_hot = (tile_row[:, 0][:, None] == lax.iota(jnp.int32, row_blocks)[None, :]).astype(
        jnp.float32
    ) * live[:, None]
    col_hot = (tile_col[:, 0][:, None] == lax.iota(jnp.int32, col_blocks)[None, :]).astype(
        jnp.float32
    )
    primal = primal_start.reshape(-1)
    dual = dual_start.reshape(-1)
    cost_flat = cost.reshape(-1)
    lower_flat = lower.reshape(-1)
    upper_flat = upper.reshape(-1)
    rhs_flat = rhs.reshape(-1)
    primal_share = primal.shape[0]
    dual_share = dual.shape[0]
    primal_full, cost_full, lower_full, upper_full = (
        lax.all_gather(primal, "row", axis=0, tiled=True),
        lax.all_gather(cost_flat, "row", axis=0, tiled=True),
        lax.all_gather(lower_flat, "row", axis=0, tiled=True),
        lax.all_gather(upper_flat, "row", axis=0, tiled=True),
    )
    dual_full, rhs_full = (
        lax.all_gather(dual, "col", axis=0, tiled=True),
        lax.all_gather(rhs_flat, "col", axis=0, tiled=True),
    )
    extrapolated = primal_full
    primal_total = jnp.zeros_like(primal_full)
    dual_total = jnp.zeros_like(dual_full)
    for iteration in range(ITERS):
        forward_taken = jnp.dot(
            col_hot, extrapolated.reshape(col_blocks, block_size), precision=exact
        )
        forward_product = jnp.einsum("tij,tj->ti", tiles, forward_taken, precision=exact)
        applied = lax.psum(
            jnp.einsum("tr,ti->ri", row_hot, forward_product, precision=exact).reshape(-1), "col"
        )
        dual_full = jnp.maximum(dual_full + dual_step * (rhs_full - applied), 0.0)
        taken = jnp.dot(row_hot, dual_full.reshape(row_blocks, block_size), precision=exact)
        product = jnp.einsum("tij,ti->tj", tiles, taken, precision=exact)
        transposed = lax.psum(
            jnp.einsum("tk,tj->kj", col_hot, product, precision=exact).reshape(-1), "row"
        )
        moved = primal_full - primal_step * (cost_full - transposed)
        primal_new = jnp.minimum(jnp.maximum(moved, lower_full), upper_full)
        extrapolated = 2.0 * primal_new - primal_full
        primal_full = primal_new
        primal_total = primal_total + primal_full
        dual_total = dual_total + dual_full
    primal_start_at = lax.axis_index("row") * primal_share
    dual_start_at = lax.axis_index("col") * dual_share
    primal = lax.dynamic_slice_in_dim(primal_full, primal_start_at, primal_share, 0)
    dual = lax.dynamic_slice_in_dim(dual_full, dual_start_at, dual_share, 0)
    primal_mean = lax.dynamic_slice_in_dim(primal_total, primal_start_at, primal_share, 0) / ITERS
    dual_mean = lax.dynamic_slice_in_dim(dual_total, dual_start_at, dual_share, 0) / ITERS
    return (
        primal_mean.reshape(1, -1),
        dual_mean.reshape(1, -1),
        primal.reshape(1, -1),
        dual.reshape(1, -1),
    )


def solution(mesh):
    return jax.shard_map(
        body,
        mesh=mesh,
        in_specs=(
            P("row", "col", None),
            P("row", "col"),
            P("row", "col"),
            P("row", "col"),
            P("col", "row"),
            P("row", "col"),
            P("col", "row"),
            P("col", "row"),
            P("col", "row"),
            P("row", "col"),
        ),
        out_specs=(P("col", "row"), P("row", "col"), P("col", "row"), P("row", "col")),
        check_vma=False,
    )
```

profile of v0, /device:TPU:0, one launch (start us, length us, event | category | flops | bytes accessed | tf_op | source)
XLA Modules:
  0.0 754.3 jit_solution(14544451130449158460)
XLA Ops:
  7.2 10.1 %all-gather = f32[1,32768]{1,0:T(1,128)S(1)} all-gather(f32[1,8192]{1,0:T(1,128)} %param.18), channel_id=2, replica_groups=mesh['row'=4,'col'=8] {'row'}, dimensions={1}, use_global_device_ids=true | all-gather | bytes 163840 | tf_op jit(solution)/shard_map/all_gather | solution.py:33
  18.1 0.9 fusion.80
  19.0 11.9 %fusion.119 = f32[96,1,128]{2,1,0:T(1,128)S(1)} fusion(f32[96,128,1]{1,2,0:T(1,128)S(1)} %bitcast.220, f32[96,128,128]{2,1,0:T(8,128)} %param.10), kind=kOutput, calls=%fused_computation.154 | convolution fusion | flops 18874368 | bytes 6389760 | tf_op jit(solution)/shard_map/tij,tj->ti/dot_general | solution.py:49
  30.8 1.4 convolution_bitcast_fusion.5
  32.3 14.5 %all-gather.3 = f32[1,65536]{1,0:T(1,128)S(1)} all-gather(f32[1,8192]{1,0:T(1,128)S(1)} %copy-done.2), channel_id=5, replica_groups=mesh['row'=4,'col'=8] {'col'}, dimensions={1}, use_global_device_ids=true | all-gather | bytes 294912 | tf_op jit(solution)/shard_map/all_gather | solution.py:40
  46.8 14.3 %all-gather.2 = f32[1,65536]{1,0:T(1,128)S(1)} all-gather(f32[1,8192]{1,0:T(1,128)S(1)} %copy-done.3), channel_id=4, replica_groups=mesh['row'=4,'col'=8] {'col'}, dimensions={1}, use_global_device_ids=true | all-gather | bytes 294912 | tf_op jit(solution)/shard_map/all_gather | solution.py:39
  61.1 27.3 %all-reduce.13.cloned.1.call-done = f32[65536]{0:T(1024)} async-done(((f32[65536]{0:T(1024)}), f32[65536]{0:T(1024)}) %all-reduce.13.cloned.1.call-update) | async-done | bytes 262160 | tf_op jit(solution)/shard_map/psum | solution.py:50
  88.3 1.0 add_maximum_fusion.5
  89.3 0.4 fusion.15
  89.7 7.3 fusion.120
  97.0 1.0 convolution_bitcast_fusion.11
  98.2 8.4 %all-gather.1 = f32[1,32768]{1,0:T(1,128)S(1)} all-gather(f32[1,8192]{1,0:T(1,128)S(1)} %copy-done.4), channel_id=3, replica_groups=mesh['row'=4,'col'=8] {'row'}, dimensions={1}, use_global_device_ids=true | all-gather | bytes 163840 | tf_op jit(solution)/shard_map/all_gather | solution.py:34
  106.6 8.5 %all-gather.4 = f32[1,32768]{1,0:T(1,128)S(1)} all-gather(f32[1,8192]{1,0:T(1,128)S(1)} %copy-done.5), channel_id=6, replica_groups=mesh['row'=4,'col'=8] {'row'}, dimensions={1}, use_global_device_ids=true | all-gather | bytes 163840 | tf_op jit(solution)/shard_map/all_gather | solution.py:35
  115.1 8.0 %all-gather.5 = f32[1,32768]{1,0:T(1,128)S(1)} all-gather(f32[1,8192]{1,0:T(1,128)S(1)} %copy-done.6), channel_id=7, replica_groups=mesh['row'=4,'col'=8] {'row'}, dimensions={1}, use_global_device_ids=true | all-gather | bytes 163840 | tf_op jit(solution)/shard_map/all_gather | solution.py:36
  123.0 16.5 %all-reduce.15.cloned.1.call-done = f32[32768]{0:T(1024)} async-done(((f32[32768]{0:T(1024)}), f32[32768]{0:T(1024)}) %all-reduce.15.cloned.1.call-update) | async-done | bytes 131088 | tf_op jit(solution)/shard_map/psum | solution.py:56
  139.6 0.9 maximum_minimum_fusion.5
  140.8 11.8 %fusion.121 = f32[96,1,128]{2,1,0:T(1,128)S(1)} fusion(f32[96,128,1]{1,2,0:T(1,128)S(1)} %bitcast.198, f32[96,128,128]{2,1,0:T(8,128)} %param.10), kind=kOutput, calls=%fused_computation.156 | convolution fusion | flops 18874368 | bytes 6389760 | tf_op jit(solution)/shard_map/tij,tj->ti/dot_general | solution.py:49
  152.6 1.4 convolution_bitcast_fusion.4
  154.1 55.5 %all-reduce.17.cloned.1.call-done = f32[65536]{0:T(1024)} async-done(((f32[65536]{0:T(1024)}), f32[65536]{0:T(1024)}) %all-reduce.17.cloned.1.call-update) | async-done | bytes 262160 | tf_op jit(solution)/shard_map/psum | solution.py:50
  209.6 1.0 add_maximum_fusion.4
  210.6 0.4 fusion.12
  210.9 7.3 fusion.122
  218.3 1.0 convolution_bitcast_fusion.10
  219.5 41.2 %all-reduce.19.cloned.1.call-done = f32[32768]{0:T(1024)} async-done(((f32[32768]{0:T(1024)}), f32[32768]{0:T(1024)}) %all-reduce.19.cloned.1.call-update) | async-done | bytes 131088 | tf_op jit(solution)/shard_map/psum | solution.py:56
  260.7 0.9 maximum_minimum_fusion.4
  261.9 11.8 %fusion.123 = f32[96,1,128]{2,1,0:T(1,128)S(1)} fusion(f32[96,128,1]{1,2,0:T(1,128)S(1)} %bitcast.207, f32[96,128,128]{2,1,0:T(8,128)} %param.10), kind=kOutput, calls=%fused_computation.158 | convolution fusion | flops 18874368 | bytes 6389760 | tf_op jit(solution)/shard_map/tij,tj->ti/dot_general | solution.py:49
  273.8 1.4 convolution_bitcast_fusion.3
  275.2 55.5 %all-reduce.21.cloned.1.call-done = f32[65536]{0:T(1024)} async-done(((f32[65536]{0:T(1024)}), f32[65536]{0:T(1024)}) %all-reduce.21.cloned.1.call-update) | async-done | bytes 262160 | tf_op jit(solution)/shard_map/psum | solution.py:50
  330.7 1.0 add_maximum_fusion.3
  331.7 0.4 fusion.9
  332.1 7.3 fusion.124
  339.5 1.0 convolution_bitcast_fusion.9
  340.6 41.4 %all-reduce.23.cloned.1.call-done = f32[32768]{0:T(1024)} async-done(((f32[32768]{0:T(1024)}), f32[32768]{0:T(1024)}) %all-reduce.23.cloned.1.call-update) | async-done | bytes 131088 | tf_op jit(solution)/shard_map/psum | solution.py:56
  381.9 0.9 maximum_minimum_fusion.3
  383.1 11.8 %fusion.125 = f32[96,1,128]{2,1,0:T(1,128)S(1)} fusion(f32[96,128,1]{1,2,0:T(1,128)S(1)} %bitcast.209, f32[96,128,128]{2,1,0:T(8,128)} %param.10), kind=kOutput, calls=%fused_computation.160 | convolution fusion | flops 18874368 | bytes 6389760 | tf_op jit(solution)/shard_map/tij,tj->ti/dot_general | solution.py:49
  395.0 1.4 convolution_bitcast_fusion.2
  396.6 55.3 %all-reduce.25.cloned.1.call-done = f32[65536]{0:T(1024)} async-done(((f32[65536]{0:T(1024)}), f32[65536]{0:T(1024)}) %all-reduce.25.cloned.1.call-update) | async-done | bytes 262160 | tf_op jit(solution)/shard_map/psum | solution.py:50
  451.9 1.0 add_maximum_fusion.2
  452.9 0.4 fusion.6
  453.3 7.3 fusion.126
  460.6 1.0 convolution_bitcast_fusion.8
  461.7 41.4 %all-reduce.27.cloned.1.call-done = f32[32768]{0:T(1024)} async-done(((f32[32768]{0:T(1024)}), f32[32768]{0:T(1024)}) %all-reduce.27.cloned.1.call-update) | async-done | bytes 131088 | tf_op jit(solution)/shard_map/psum | solution.py:56
  503.1 0.9 maximum_minimum_fusion.2
  504.3 11.8 %fusion.127 = f32[96,1,128]{2,1,0:T(1,128)S(1)} fusion(f32[96,128,1]{1,2,0:T(1,128)S(1)} %bitcast.211, f32[96,128,128]{2,1,0:T(8,128)} %param.10), kind=kOutput, calls=%fused_computation.162 | convolution fusion | flops 18874368 | bytes 6389760 | tf_op jit(solution)/shard_map/tij,tj->ti/dot_general | solution.py:49
  516.1 1.4 convolution_bitcast_fusion.1
  517.6 55.5 %all-reduce.29.cloned.1.call-done = f32[65536]{0:T(1024)} async-done(((f32[65536]{0:T(1024)}), f32[65536]{0:T(1024)}) %all-reduce.29.cloned.1.call-update) | async-done | bytes 262160 | tf_op jit(solution)/shard_map/psum | solution.py:50
  573.1 1.0 add_maximum_fusion.1
  574.1 0.4 fusion.3
  574.5 7.3 fusion.128
  581.8 1.0 convolution_bitcast_fusion.7
  582.9 0.3 all-reduce.33.cloned.1.call-start
  583.2 41.1 %all-reduce.31.cloned.1.call-done = f32[32768]{0:T(1024)} async-done(((f32[32768]{0:T(1024)}), f32[32768]{0:T(1024)}) %all-reduce.31.cloned.1.call-update) | async-done | bytes 131088 | tf_op jit(solution)/shard_map/psum | solution.py:56
  624.3 0.9 maximum_minimum_fusion.1
  625.5 11.8 %fusion.129 = f32[96,1,128]{2,1,0:T(1,128)S(1)} fusion(f32[96,128,1]{1,2,0:T(1,128)S(1)} %bitcast.213, f32[96,128,128]{2,1,0:T(8,128)} %param.10), kind=kOutput, calls=%fused_computation.164 | convolution fusion | flops 18874368 | bytes 6389760 | tf_op jit(solution)/shard_map/tij,tj->ti/dot_general | solution.py:49
  637.3 1.4 convolution_bitcast_fusion
  638.8 55.5 %all-reduce.33.cloned.1.call-done = f32[65536]{0:T(1024)} async-done(((f32[65536]{0:T(1024)}), f32[65536]{0:T(1024)}) %all-reduce.33.cloned.1.call-update) | async-done | bytes 262160 | tf_op jit(solution)/shard_map/psum | solution.py:50
  694.3 1.0 add_maximum_fusion
  695.3 0.4 fusion
  695.7 7.3 fusion.130
  703.0 1.0 convolution_bitcast_fusion.6
  704.0 0.6 fusion.99
  704.7 40.8 %all-reduce.35.cloned.1.call-done = f32[32768]{0:T(1024)} async-done(((f32[32768]{0:T(1024)}), f32[32768]{0:T(1024)}) %all-reduce.35.cloned.1.call-update) | async-done | bytes 131088 | tf_op jit(solution)/shard_map/psum | solution.py:56
  745.5 0.9 maximum_minimum_fusion
  746.4 0.6 fusion.101
  (43 shorter events, 2.3 us)
Async XLA Ops:
  7.2 23.7 %copy-start = (s32[96,1]{0,1:T(1,128)S(1)}, s32[96,1]{0,1:T(1,128)}, u32[]{:S(2)}) copy-start(s32[96,1]{0,1:T(1,128)} %param.11) | copy-start | bytes 1156
  7.2 25.1 %copy-start.2 = (f32[1,8192]{1,0:T(1,128)S(1)}, f32[1,8192]{1,0:T(1,128)}, u32[]{:S(2)}) copy-start(f32[1,8192]{1,0:T(1,128)} %param.15) | copy-start | bytes 98308
  7.2 39.6 %copy-start.3 = (f32[1,8192]{1,0:T(1,128)S(1)}, f32[1,8192]{1,0:T(1,128)}, u32[]{:S(2)}) copy-start(f32[1,8192]{1,0:T(1,128)} %param.19) | copy-start | bytes 98308
  7.2 81.1 %all-reduce.13.cloned.1.call-start = ((), (), s32[]{:S(2)}) async-start(), calls=%async_computation | async-start | bytes 524288 | tf_op jit(solution)/shard_map/psum | solution.py:50
  18.9 78.1 %copy-start.1 = (s32[96,1]{0,1:T(1,128)S(1)}, s32[96,1]{0,1:T(1,128)}, u32[]{:S(2)}) copy-start(s32[96,1]{0,1:T(1,128)} %param.12) | copy-start | bytes 1156
  19.0 79.2 %copy-start.4 = (f32[1,8192]{1,0:T(1,128)S(1)}, f32[1,8192]{1,0:T(1,128)}, u32[]{:S(2)}) copy-start(f32[1,8192]{1,0:T(1,128)} %param.14) | copy-start | bytes 98308
  30.8 75.8 %copy-start.5 = (f32[1,8192]{1,0:T(1,128)S(1)}, f32[1,8192]{1,0:T(1,128)}, u32[]{:S(2)}) copy-start(f32[1,8192]{1,0:T(1,128)} %param.16) | copy-start | bytes 98308
  30.8 84.2 %copy-start.6 = (f32[1,8192]{1,0:T(1,128)S(1)}, f32[1,8192]{1,0:T(1,128)}, u32[]{:S(2)}) copy-start(f32[1,8192]{1,0:T(1,128)} %param.17) | copy-start | bytes 98308
  32.2 107.3 %all-reduce.15.cloned.1.call-start = ((), (), s32[]{:S(2)}) async-start(), calls=%async_computation.1 | async-start | bytes 262144 | tf_op jit(solution)/shard_map/psum | solution.py:56
  98.1 111.5 %all-reduce.17.cloned.1.call-start = ((), (), s32[]{:S(2)}) async-start(), calls=%async_computation.2 | async-start | bytes 524288 | tf_op jit(solution)/shard_map/psum | solution.py:50
  154.0 106.7 %all-reduce.19.cloned.1.call-start = ((), (), s32[]{:S(2)}) async-start(), calls=%async_computation.3 | async-start | bytes 262144 | tf_op jit(solution)/shard_map/psum | solution.py:56
  219.3 111.4 %all-reduce.21.cloned.1.call-start = ((), (), s32[]{:S(2)}) async-start(), calls=%async_computation.4 | async-start | bytes 524288 | tf_op jit(solution)/shard_map/psum | solution.py:50
  275.2 106.7 %all-reduce.23.cloned.1.call-start = ((), (), s32[]{:S(2)}) async-start(), calls=%async_computation.5 | async-start | bytes 262144 | tf_op jit(solution)/shard_map/psum | solution.py:56
  340.5 111.4 %all-reduce.25.cloned.1.call-start = ((), (), s32[]{:S(2)}) async-start(), calls=%async_computation.6 | async-start | bytes 524288 | tf_op jit(solution)/shard_map/psum | solution.py:50
  396.4 106.7 %all-reduce.27.cloned.1.call-start = ((), (), s32[]{:S(2)}) async-start(), calls=%async_computation.7 | async-start | bytes 262144 | tf_op jit(solution)/shard_map/psum | solution.py:56
  461.7 111.4 %all-reduce.29.cloned.1.call-start = ((), (), s32[]{:S(2)}) async-start(), calls=%async_computation.8 | async-start | bytes 524288 | tf_op jit(solution)/shard_map/psum | solution.py:50
  517.5 106.7 %all-reduce.31.cloned.1.call-start = ((), (), s32[]{:S(2)}) async-start(), calls=%async_computation.9 | async-start | bytes 262144 | tf_op jit(solution)/shard_map/psum | solution.py:56
  582.9 111.4 %all-reduce.33.cloned.1.call-start = ((), (), s32[]{:S(2)}) async-start(), calls=%async_computation.10 | async-start | bytes 524288 | tf_op jit(solution)/shard_map/psum | solution.py:50
  638.7 106.7 %all-reduce.35.cloned.1.call-start = ((), (), s32[]{:S(2)}) async-start(), calls=%async_computation.11 | async-start | bytes 262144 | tf_op jit(solution)/shard_map/psum | solution.py:56
Sparse Core Ops, SparseCore 0:
  32.4 55.9 all-reduce.12
  98.2 41.3 all-reduce.14
  154.1 55.4 all-reduce.16
  219.4 41.2 all-reduce.18
  275.3 55.4 all-reduce.20
  340.6 41.2 all-reduce.22
  396.5 55.4 all-reduce.24
  461.8 41.2 all-reduce.26
  517.7 55.4 all-reduce.28
  583.0 41.2 all-reduce.30
  638.8 55.4 all-reduce.32
  704.2 41.2 all-reduce.34
where the time goes:
time: 762 us; the launch traced here: 754 us
  waiting for transfers between devices  527 us (69%)
  matrix products  134 us (18%)
  blocking collectives  63.8 us (8%)
  between operations  15.5 us (2%)
  other arithmetic  12.9 us (2%)
    psum x6, waiting for transfers between devices, body(): lax.psum(jnp.einsum('tr,ti->ri', row_hot, forward_product, precision=exac...  305 us
    psum x6, waiting for transfers between devices, body(): lax.psum(jnp.einsum('tk,tj->kj', col_hot, product, precision=exact).resha...  222 us
    dot_general x6, matrix products, body(): jnp.einsum('tij,tj->ti', tiles, forward_taken, precision=exact)  71.1 us
    dot_general x6, matrix products, body(): product = jnp.einsum('tij,ti->tj', tiles, taken, precision=exact)  43.9 us
  transfers between devices with their start and end apart: 12, of which 12 were waited for; matrix products, arithmetic and copies ran while one was open for 0% of the time, Pallas kernels for 0%

commit v1 on v0

--- a/solution.py
+++ b/solution.py
@@ -53,8 +53,11 @@
         dual_full = jnp.maximum(dual_full + dual_step * (rhs_full - applied), 0.0)
         taken = jnp.dot(row_hot, dual_full.reshape(row_blocks, block_size), precision=exact)
         product = jnp.einsum("tij,ti->tj", tiles, taken, precision=exact)
-        transposed = lax.psum(
-            jnp.einsum("tk,tj->kj", col_hot, product, precision=exact).reshape(-1), "row"
+        transposed = jnp.sum(
+            lax.all_gather(
+                jnp.einsum("tk,tj->kj", col_hot, product, precision=exact).reshape(-1), "row"
+            ),
+            axis=0,
         )
         moved = primal_full - primal_step * (cost_full - transposed)
         primal_new = jnp.minimum(jnp.maximum(moved, lower_full), upper_full)

time: 762 us -> 564 us (0.74)
  waiting for transfers between devices: 527 us -> 271 us
  blocking collectives: 63.8 us -> 129 us
    psum x6 -> x0, waiting for transfers between devices: 222 us -> none  [body(): lax.psum(jnp.einsum('tk,tj->kj', col_hot, product, precision=exact).resha...]
    all_gather x0 -> x6, blocking collectives: none -> 65.5 us  [body(): lax.all_gather(jnp.einsum('tk,tj->kj', col_hot, product, precision=exact)...]
    psum x6, waiting for transfers between devices: 305 us -> 271 us  [body(): lax.psum(jnp.einsum('tr,ti->ri', row_hot, forward_product, precision=exac...]
  transfers between devices with their start and end apart: 12 -> 6, of which waited for: 12 -> 6; matrix products, arithmetic and copies ran while one was open for 0% -> 0% of each run, Pallas kernels for 0% -> 0%
where the time goes in v1:
time: 564 us; the launch traced here: 556 us
  waiting for transfers between devices  271 us (48%)
  matrix products  130 us (23%)
  blocking collectives  129 us (23%)
  between operations  15.6 us (3%)
  other arithmetic  10.4 us (2%)
    psum x6, waiting for transfers between devices, body(): lax.psum(jnp.einsum('tr,ti->ri', row_hot, forward_product, precision=exac...  271 us
    dot_general x6, matrix products, body(): jnp.einsum('tij,tj->ti', tiles, forward_taken, precision=exact)  71.1 us
    all_gather x6, blocking collectives, body(): lax.all_gather(jnp.einsum('tk,tj->kj', col_hot, product, precision=exact)...  65.5 us
    dot_general x6, matrix products, body(): product = jnp.einsum('tij,ti->tj', tiles, taken, precision=exact)  43.9 us
    all_gather x1, blocking collectives, body(): lax.all_gather(rhs_flat, 'col', axis=0, tiled=True)  14.5 us
    all_gather x1, blocking collectives, body(): lax.all_gather(dual, 'col', axis=0, tiled=True)  14.5 us
  transfers between devices with their start and end apart: 6, of which 6 were waited for; matrix products, arithmetic and copies ran while one was open for 0% of the time, Pallas kernels for 0%

profile of v1, /device:TPU:0, one launch (start us, length us, event | category | flops | bytes accessed | tf_op | source)
XLA Modules:
  0.0 556.2 jit_solution(3669220493312321887)
XLA Ops:
  7.3 10.1 %all-gather = f32[1,32768]{1,0:T(1,128)S(1)} all-gather(f32[1,8192]{1,0:T(1,128)} %param.18), channel_id=2, replica_groups=mesh['row'=4,'col'=8] {'row'}, dimensions={1}, use_global_device_ids=true | all-gather | bytes 163840 | tf_op jit(solution)/shard_map/all_gather | solution.py:33
  18.1 0.9 fusion.86
  19.0 11.8 %fusion.125 = f32[96,1,128]{2,1,0:T(1,128)S(1)} fusion(f32[96,128,1]{1,2,0:T(1,128)S(1)} %bitcast.220, f32[96,128,128]{2,1,0:T(8,128)} %param.10), kind=kOutput, calls=%fused_computation.154 | convolution fusion | flops 18874368 | bytes 6389760 | tf_op jit(solution)/shard_map/tij,tj->ti/dot_general | solution.py:49
  30.8 1.4 convolution_bitcast_fusion.5
  32.3 14.5 %all-gather.3 = f32[1,65536]{1,0:T(1,128)S(1)} all-gather(f32[1,8192]{1,0:T(1,128)S(1)} %copy-done.2), channel_id=5, replica_groups=mesh['row'=4,'col'=8] {'col'}, dimensions={1}, use_global_device_ids=true | all-gather | bytes 294912 | tf_op jit(solution)/shard_map/all_gather | solution.py:40
  46.8 8.2 %all-gather.1 = f32[1,32768]{1,0:T(1,128)S(1)} all-gather(f32[1,8192]{1,0:T(1,128)S(1)} %copy-done.3), channel_id=3, replica_groups=mesh['row'=4,'col'=8] {'row'}, dimensions={1}, use_global_device_ids=true | all-gather | bytes 163840 | tf_op jit(solution)/shard_map/all_gather | solution.py:34
  55.0 7.9 %all-gather.4 = f32[1,32768]{1,0:T(1,128)S(1)} all-gather(f32[1,8192]{1,0:T(1,128)S(1)} %copy-done.4), channel_id=6, replica_groups=mesh['row'=4,'col'=8] {'row'}, dimensions={1}, use_global_device_ids=true | all-gather | bytes 163840 | tf_op jit(solution)/shard_map/all_gather | solution.py:35
  62.9 8.0 %all-gather.5 = f32[1,32768]{1,0:T(1,128)S(1)} all-gather(f32[1,8192]{1,0:T(1,128)S(1)} %copy-done.5), channel_id=7, replica_groups=mesh['row'=4,'col'=8] {'row'}, dimensions={1}, use_global_device_ids=true | all-gather | bytes 163840 | tf_op jit(solution)/shard_map/all_gather | solution.py:36
  70.9 14.5 %all-gather.2 = f32[1,65536]{1,0:T(1,128)S(1)} all-gather(f32[1,8192]{1,0:T(1,128)S(1)} %copy-done.6), channel_id=4, replica_groups=mesh['row'=4,'col'=8] {'col'}, dimensions={1}, use_global_device_ids=true | all-gather | bytes 294912 | tf_op jit(solution)/shard_map/all_gather | solution.py:39
  85.4 3.0 all-reduce.7.cloned.1.call-done
  88.3 1.0 add_maximum_fusion.5
  89.3 0.4 fusion.15
  89.7 7.3 %fusion.126 = f32[96,1,128]{2,1,0:T(1,128)S(1)} fusion(f32[96,128,1]{1,2,0:T(1,128)S(1)} %bitcast.205, f32[96,128,128]{2,1,0:T(8,128)} %param.10), kind=kOutput, calls=%fused_computation.155 | convolution fusion | flops 18874368 | bytes 6389760 | tf_op jit(solution)/shard_map/tij,ti->tj/dot_general | solution.py:55
  97.0 0.4 fusion.85
  97.4 11.1 %all-gather.6 = f32[4,1,32768]{2,1,0:T(1,128)S(1)} all-gather(f32[1,1,32768]{2,1,0:T(1,128)S(1)} %bitcast.191), channel_id=1, replica_groups=mesh['row'=4,'col'=8] {'row'}, dimensions={0}, use_global_device_ids=true | all-gather | bytes 655360 | tf_op jit(solution)/shard_map/all_gather | solution.py:57
  108.5 0.5 reduce_sum.54
  109.3 11.8 %fusion.127 = f32[96,1,128]{2,1,0:T(1,128)S(1)} fusion(f32[96,128,1]{1,2,0:T(1,128)S(1)} %bitcast.199, f32[96,128,128]{2,1,0:T(8,128)} %param.10), kind=kOutput, calls=%fused_computation.156 | convolution fusion | flops 18874368 | bytes 6389760 | tf_op jit(solution)/shard_map/tij,tj->ti/dot_general | solution.py:49
  121.1 1.4 convolution_bitcast_fusion.4
  122.6 53.7 %all-reduce.9.cloned.1.call-done = f32[65536]{0:T(1024)} async-done(((f32[65536]{0:T(1024)}), f32[65536]{0:T(1024)}) %all-reduce.9.cloned.1.call-update) | async-done | bytes 262160 | tf_op jit(solution)/shard_map/psum | solution.py:50
  176.3 1.0 add_maximum_fusion.4
  177.3 0.4 fusion.12
  177.7 7.3 %fusion.128 = f32[96,1,128]{2,1,0:T(1,128)S(1)} fusion(f32[96,128,1]{1,2,0:T(1,128)S(1)} %bitcast.206, f32[96,128,128]{2,1,0:T(8,128)} %param.10), kind=kOutput, calls=%fused_computation.157 | convolution fusion | flops 18874368 | bytes 6389760 | tf_op jit(solution)/shard_map/tij,ti->tj/dot_general | solution.py:55
  185.0 0.4 fusion.84
  185.4 10.9 %all-gather.7 = f32[4,1,32768]{2,1,0:T(1,128)S(1)} all-gather(f32[1,1,32768]{2,1,0:T(1,128)S(1)} %bitcast.192), channel_id=1, replica_groups=mesh['row'=4,'col'=8] {'row'}, dimensions={0}, use_global_device_ids=true | all-gather | bytes 655360 | tf_op jit(solution)/shard_map/all_gather | solution.py:57
  196.2 0.5 reduce_sum.55
  197.0 11.8 %fusion.129 = f32[96,1,128]{2,1,0:T(1,128)S(1)} fusion(f32[96,128,1]{1,2,0:T(1,128)S(1)} %bitcast.207, f32[96,128,128]{2,1,0:T(8,128)} %param.10), kind=kOutput, calls=%fused_computation.158 | convolution fusion | flops 18874368 | bytes 6389760 | tf_op jit(solution)/shard_map/tij,tj->ti/dot_general | solution.py:49
  208.8 1.4 convolution_bitcast_fusion.3
  210.3 53.7 %all-reduce.11.cloned.1.call-done = f32[65536]{0:T(1024)} async-done(((f32[65536]{0:T(1024)}), f32[65536]{0:T(1024)}) %all-reduce.11.cloned.1.call-update) | async-done | bytes 262160 | tf_op jit(solution)/shard_map/psum | solution.py:50
  264.0 1.0 add_maximum_fusion.3
  265.0 0.4 fusion.9
  265.3 7.3 %fusion.130 = f32[96,1,128]{2,1,0:T(1,128)S(1)} fusion(f32[96,128,1]{1,2,0:T(1,128)S(1)} %bitcast.208, f32[96,128,128]{2,1,0:T(8,128)} %param.10), kind=kOutput, calls=%fused_computation.159 | convolution fusion | flops 18874368 | bytes 6389760 | tf_op jit(solution)/shard_map/tij,ti->tj/dot_general | solution.py:55
  272.7 0.4 fusion.83
  273.0 10.9 %all-gather.8 = f32[4,1,32768]{2,1,0:T(1,128)S(1)} all-gather(f32[1,1,32768]{2,1,0:T(1,128)S(1)} %bitcast.193), channel_id=1, replica_groups=mesh['row'=4,'col'=8] {'row'}, dimensions={0}, use_global_device_ids=true | all-gather | bytes 655360 | tf_op jit(solution)/shard_map/all_gather | solution.py:57
  284.0 0.5 reduce_sum.56
  284.7 11.8 %fusion.131 = f32[96,1,128]{2,1,0:T(1,128)S(1)} fusion(f32[96,128,1]{1,2,0:T(1,128)S(1)} %bitcast.209, f32[96,128,128]{2,1,0:T(8,128)} %param.10), kind=kOutput, calls=%fused_computation.160 | convolution fusion | flops 18874368 | bytes 6389760 | tf_op jit(solution)/shard_map/tij,tj->ti/dot_general | solution.py:49
  296.6 1.4 convolution_bitcast_fusion.2
  298.0 53.7 %all-reduce.13.cloned.1.call-done = f32[65536]{0:T(1024)} async-done(((f32[65536]{0:T(1024)}), f32[65536]{0:T(1024)}) %all-reduce.13.cloned.1.call-update) | async-done | bytes 262160 | tf_op jit(solution)/shard_map/psum | solution.py:50
  351.7 1.0 add_maximum_fusion.2
  352.7 0.4 fusion.6
  353.1 7.3 %fusion.132 = f32[96,1,128]{2,1,0:T(1,128)S(1)} fusion(f32[96,128,1]{1,2,0:T(1,128)S(1)} %bitcast.210, f32[96,128,128]{2,1,0:T(8,128)} %param.10), kind=kOutput, calls=%fused_computation.161 | convolution fusion | flops 18874368 | bytes 6389760 | tf_op jit(solution)/shard_map/tij,ti->tj/dot_general | solution.py:55
  360.4 0.4 fusion.82
  360.8 11.0 %all-gather.9 = f32[4,1,32768]{2,1,0:T(1,128)S(1)} all-gather(f32[1,1,32768]{2,1,0:T(1,128)S(1)} %bitcast.194), channel_id=1, replica_groups=mesh['row'=4,'col'=8] {'row'}, dimensions={0}, use_global_device_ids=true | all-gather | bytes 655360 | tf_op jit(solution)/shard_map/all_gather | solution.py:57
  371.7 0.5 reduce_sum.57
  372.2 0.2 fusion.26
  372.5 11.8 %fusion.133 = f32[96,1,128]{2,1,0:T(1,128)S(1)} fusion(f32[96,128,1]{1,2,0:T(1,128)S(1)} %bitcast.211, f32[96,128,128]{2,1,0:T(8,128)} %param.10), kind=kOutput, calls=%fused_computation.162 | convolution fusion | flops 18874368 | bytes 6389760 | tf_op jit(solution)/shard_map/tij,tj->ti/dot_general | solution.py:49
  384.3 1.4 convolution_bitcast_fusion.1
  385.8 53.7 %all-reduce.15.cloned.1.call-done = f32[65536]{0:T(1024)} async-done(((f32[65536]{0:T(1024)}), f32[65536]{0:T(1024)}) %all-reduce.15.cloned.1.call-update) | async-done | bytes 262160 | tf_op jit(solution)/shard_map/psum | solution.py:50
  439.5 1.0 add_maximum_fusion.1
  440.5 0.4 fusion.3
  440.8 7.3 %fusion.134 = f32[96,1,128]{2,1,0:T(1,128)S(1)} fusion(f32[96,128,1]{1,2,0:T(1,128)S(1)} %bitcast.212, f32[96,128,128]{2,1,0:T(8,128)} %param.10), kind=kOutput, calls=%fused_computation.163 | convolution fusion | flops 18874368 | bytes 6389760 | tf_op jit(solution)/shard_map/tij,ti->tj/dot_general | solution.py:55
  448.2 0.4 fusion.81
  448.5 11.0 %all-gather.10 = f32[4,1,32768]{2,1,0:T(1,128)S(1)} all-gather(f32[1,1,32768]{2,1,0:T(1,128)S(1)} %bitcast.195), channel_id=1, replica_groups=mesh['row'=4,'col'=8] {'row'}, dimensions={0}, use_global_device_ids=true | all-gather | bytes 655360 | tf_op jit(solution)/shard_map/all_gather | solution.py:57
  459.5 0.5 reduce_sum.58
  460.3 11.8 %fusion.135 = f32[96,1,128]{2,1,0:T(1,128)S(1)} fusion(f32[96,128,1]{1,2,0:T(1,128)S(1)} %bitcast.213, f32[96,128,128]{2,1,0:T(8,128)} %param.10), kind=kOutput, calls=%fused_computation.164 | convolution fusion | flops 18874368 | bytes 6389760 | tf_op jit(solution)/shard_map/tij,tj->ti/dot_general | solution.py:49
  472.1 1.4 convolution_bitcast_fusion
  473.6 53.7 %all-reduce.17.cloned.1.call-done = f32[65536]{0:T(1024)} async-done(((f32[65536]{0:T(1024)}), f32[65536]{0:T(1024)}) %all-reduce.17.cloned.1.call-update) | async-done | bytes 262160 | tf_op jit(solution)/shard_map/psum | solution.py:50
  527.3 1.0 add_maximum_fusion
  528.3 0.4 fusion
  528.6 0.6 fusion.105
  529.3 7.3 %fusion.136 = f32[96,1,128]{2,1,0:T(1,128)S(1)} fusion(f32[96,128,1]{1,2,0:T(1,128)S(1)} %bitcast.197, f32[96,128,128]{2,1,0:T(8,128)} %param.10), kind=kOutput, calls=%fused_computation.165 | convolution fusion | flops 18874368 | bytes 6389760 | tf_op jit(solution)/shard_map/tij,ti->tj/dot_general | solution.py:55
  536.6 0.4 fusion.80
  537.0 10.7 %all-gather.11 = f32[4,1,32768]{2,1,0:T(1,128)S(1)} all-gather(f32[1,1,32768]{2,1,0:T(1,128)S(1)} %bitcast.196), channel_id=1, replica_groups=mesh['row'=4,'col'=8] {'row'}, dimensions={0}, use_global_device_ids=true | all-gather | bytes 655360 | tf_op jit(solution)/shard_map/all_gather | solution.py:57
  547.7 0.5 reduce_sum.59
  548.2 0.6 fusion.107
  (37 shorter events, 1.5 us)
Async XLA Ops:
  7.2 23.7 %copy-start = (s32[96,1]{0,1:T(1,128)S(1)}, s32[96,1]{0,1:T(1,128)}, u32[]{:S(2)}) copy-start(s32[96,1]{0,1:T(1,128)} %param.11) | copy-start | bytes 1156
  7.2 25.1 %copy-start.2 = (f32[1,8192]{1,0:T(1,128)S(1)}, f32[1,8192]{1,0:T(1,128)}, u32[]{:S(2)}) copy-start(f32[1,8192]{1,0:T(1,128)} %param.15) | copy-start | bytes 98308
  7.2 39.6 %copy-start.3 = (f32[1,8192]{1,0:T(1,128)S(1)}, f32[1,8192]{1,0:T(1,128)}, u32[]{:S(2)}) copy-start(f32[1,8192]{1,0:T(1,128)} %param.14) | copy-start | bytes 98308
  7.2 47.8 %copy-start.4 = (f32[1,8192]{1,0:T(1,128)S(1)}, f32[1,8192]{1,0:T(1,128)}, u32[]{:S(2)}) copy-start(f32[1,8192]{1,0:T(1,128)} %param.16) | copy-start | bytes 98308
  7.2 55.7 %copy-start.5 = (f32[1,8192]{1,0:T(1,128)S(1)}, f32[1,8192]{1,0:T(1,128)}, u32[]{:S(2)}) copy-start(f32[1,8192]{1,0:T(1,128)} %param.17) | copy-start | bytes 98308
  7.2 63.7 %copy-start.6 = (f32[1,8192]{1,0:T(1,128)S(1)}, f32[1,8192]{1,0:T(1,128)}, u32[]{:S(2)}) copy-start(f32[1,8192]{1,0:T(1,128)} %param.19) | copy-start | bytes 98308
  7.2 81.1 %all-reduce.7.cloned.1.call-start = ((), (), s32[]{:S(2)}) async-start(), calls=%async_computation | async-start | bytes 524288 | tf_op jit(solution)/shard_map/psum | solution.py:50
  30.8 66.2 %copy-start.1 = (s32[96,1]{0,1:T(1,128)S(1)}, s32[96,1]{0,1:T(1,128)}, u32[]{:S(2)}) copy-start(s32[96,1]{0,1:T(1,128)} %param.12) | copy-start | bytes 1156
  32.2 144.0 %all-reduce.9.cloned.1.call-start = ((), (), s32[]{:S(2)}) async-start(), calls=%async_computation.1 | async-start | bytes 524288 | tf_op jit(solution)/shard_map/psum | solution.py:50
  122.5 141.4 %all-reduce.11.cloned.1.call-start = ((), (), s32[]{:S(2)}) async-start(), calls=%async_computation.2 | async-start | bytes 524288 | tf_op jit(solution)/shard_map/psum | solution.py:50
  210.3 141.4 %all-reduce.13.cloned.1.call-start = ((), (), s32[]{:S(2)}) async-start(), calls=%async_computation.3 | async-start | bytes 524288 | tf_op jit(solution)/shard_map/psum | solution.py:50
  298.0 141.5 %all-reduce.15.cloned.1.call-start = ((), (), s32[]{:S(2)}) async-start(), calls=%async_computation.4 | async-start | bytes 524288 | tf_op jit(solution)/shard_map/psum | solution.py:50
  385.7 141.5 %all-reduce.17.cloned.1.call-start = ((), (), s32[]{:S(2)}) async-start(), calls=%async_computation.5 | async-start | bytes 524288 | tf_op jit(solution)/shard_map/psum | solution.py:50
Sparse Core Ops, SparseCore 0:
  32.4 55.9 all-reduce.6
  122.7 53.5 all-reduce.8
  210.4 53.5 all-reduce.10
  298.1 53.5 all-reduce.12
  385.9 53.5 all-reduce.14
  473.7 53.5 all-reduce.16
